TPU v7x, 32 devices: a whole 2x2x4 slice. The times are simulated.
32 devices in a mesh: grp: 4 (over x, core), col: 8 (over z, y).
Axes of the slice: x: 2, y: 2, z: 4, core: 2. Of those that a mesh axis runs over, the one named last changes fastest.
Arguments:
- diag_blocks: float32 [4096, 1024], P('grp', 'col'), may hold values from -8 to 48, as said below
- coupling: float32 [24576, 1024], P(('grp', 'col')), may hold values from -4 to 4
- parent_front: float32 [12288, 12288], P('grp', 'col'), may hold values from -6 to 6
- index_maps: int32 [4, 48], replicated, may hold values from 0 to 95, as said below
Outputs:
- assembled: float32 [12288, 12288], P('grp', 'col')
- diag_factor: float32 [4096, 1024], P('grp', 'col')
- panel: float32 [24576, 1024], P(('grp', 'col'))
Inputs may be any that keep to these rules, and one draw needn't show every extreme that they name: `diag_blocks`: each front's block of 1024 rows is symmetric positive definite. `index_maps`: the 48 entries of one row are distinct, and every parent block is named by some front.
All inputs are finite; a program needn't handle non-finite values.
Results may differ from a plain program's by a relative error of at most 0.0027.
Values may be sent and summed in bfloat16 or wider, within the bound.
No kernel may reach another device: no remote copies, remote signals or barrier semaphores. Data moves between devices by JAX's collectives and lax.ppermute only.
A program may use at most 192 MiB of HBM per device.

v0:
```python
import jax
import jax.numpy as jnp
from jax import lax
from jax.sharding import PartitionSpec as P

FRONTS = 4
BLK = 128
SBLK = 48
PBLK = 96


def swapped(block, axis, stride):
    count = lax.axis_size(axis)
    route = []
    for low in range(count):
        high = low | 1 << stride
        if high != low and high < count:
            route += [(low, high), (high, low)]
    return lax.ppermute(block, axis, route)


def place_rows(slab_blocks, source_block, present_count, count):
    picked = slab_blocks[jnp.arange(FRONTS)[:, None], source_block]
    picked = jnp.where(present_count[:, :, None, None] > 0, picked, jnp.zeros_like(picked))
    return jnp.transpose(picked, (1, 2, 0, 3)).reshape(count * BLK, -1)


def on_device(diag_blocks, coupling, parent_front, index_maps):
    groups = lax.axis_size("grp") // FRONTS
    swap_depth = groups.bit_length() - 1
    grp_index = lax.axis_index("grp")
    col_index = lax.axis_index("col")
    gathered = lax.all_gather(diag_blocks, "col", axis=1, tiled=True)
    for bit_pos in range(swap_depth):
        partner = swapped(gathered, "grp", bit_pos)
        is_upper = grp_index // 2**bit_pos % 2 == 1
        lower_half = jnp.where(is_upper, partner, gathered)
        upper_half = jnp.where(is_upper, gathered, partner)
        gathered = jnp.concatenate([lower_half, upper_half], axis=0)
    factor = jnp.linalg.cholesky(gathered)
    rows_here = diag_blocks.shape[0]
    col_width = diag_blocks.shape[1]
    local_start = grp_index % groups * rows_here
    factor_tile = lax.dynamic_slice(
        factor, (local_start, col_index * col_width), (rows_here, col_width)
    )
    panel_rows = lax.linalg.triangular_solve(
        factor, coupling, left_side=False, lower=True, transpose_a=True
    )
    panel_half = panel_rows.astype(jnp.bfloat16)
    panel_tiles = lax.all_to_all(panel_half, "col", split_axis=1, concat_axis=0, tiled=True)
    panel_slab = lax.all_gather(panel_tiles, "grp", axis=0, tiled=True)
    slab_blocks = panel_slab.reshape(FRONTS, SBLK, BLK, -1)
    parent_ids = jnp.arange(PBLK, dtype=jnp.int32)
    matches = (index_maps[:, :, None] == parent_ids[None, None, :]).astype(jnp.int32)
    present_count = jnp.sum(matches, axis=1)
    source_block = jnp.sum(matches * jnp.arange(SBLK, dtype=jnp.int32)[None, :, None], axis=1)
    row_count = parent_front.shape[0]
    contract = (((1,), (1,)), ((), ()))
    every_part = place_rows(slab_blocks, source_block, present_count, PBLK)
    col_operand = lax.all_to_all(every_part, "col", split_axis=0, concat_axis=1, tiled=True)
    row_part = lax.dynamic_slice_in_dim(every_part, grp_index * row_count, row_count, 0)
    update = lax.dot_general(
        lax.all_gather(row_part, "col", axis=1, tiled=True),
        col_operand,
        contract,
        preferred_element_type=jnp.float32,
    )
    merged = parent_front - update
    return (merged, factor_tile, panel_rows)


def solution(mesh):
    in_specs = (P("grp", "col"), P(("grp", "col"), None), P("grp", "col"), P())
    out_specs = (P("grp", "col"), P("grp", "col"), P(("grp", "col"), None))
    return jax.shard_map(
        on_device, mesh=mesh, in_specs=in_specs, out_specs=out_specs, check_vma=False
    )
```

profile of v0, /device:TPU:29, one launch (start us, length us, event | category | flops | bytes accessed | tf_op | source)
XLA Modules:
  0.0 1300.4 jit_solution(12328912837952660922)
XLA Ops:
  9.3 72.7 %all-gather.4.cloned.1.call-done = f32[1024,1024]{0,1:T(8,128)} async-done(((f32[1024,128]{0,1:T(8,128)}), f32[1024,1024]{0,1:T(8,128)}) %all-gather.4.cloned.1.call-update) | async-done | bytes 4194320 | tf_op jit(solution)/shard_map/all_gather | solution.py:33
  93.7 11.7 cholesky.223
  105.5 9.8 custom-call.62
  121.7 12.2 cholesky.244
  134.5 9.8 custom-call.63
  147.6 11.7 cholesky.468
  160.7 9.8 custom-call.64
  174.0 11.8 cholesky.487
  187.2 9.8 custom-call.65
  200.4 11.7 cholesky.506
  213.4 10.0 custom-call.66
  226.7 11.7 cholesky.526
  239.7 9.8 custom-call.67
  252.5 12.1 cholesky.546
  265.9 9.8 custom-call.68
  278.5 11.7 cholesky.564
  297.2 6.9 fusion.1
  304.1 29.0 %while.1 = (s32[]{:T(128)}, f32[1024,1024]{1,0:T(8,128)}, s32[8,2]{0,1:T(2,128)S(1)}, f32[8,128,128]{2,1,0:T(8,128)}, s32[]{:T(128)}) while((s32[]{:T(128)}, f32[1024,1024]{1,0:T(8,128)}, s32[8,2]{0,1:T(2,128)S(1)}, f32[8,128,128]{2,1,0:T(8,128)}, s32[]{:T(128)}) %tuple.72), condition=%wide.while_cond, body=%wide.while_body.sunk | while | flops 2 | bytes 132205 | solution.py:47
  333.2 80.2 %custom-call.69 = f32[8,128,128]{1,2,0:T(8,128)} custom-call(f32[8,128,128]{2,1,0:T(8,128)} %get-tuple-element.10), custom_call_target="InvertDiagBlocksLowerTriangular" | custom-call | tf_op jit(solution)/shard_map/triangular_solve | solution.py:47
  438.9 6.0 convolution_subtract_fusion.2
  445.4 40.0 %all_to_all.35 = bf16[768,8,128]{0,2,1:T(8,128)(2,1)S(1)} all-to-all(bf16[768,8,128]{0,2,1:T(8,128)(2,1)S(1)} %get-tuple-element.103), channel_id=1, replica_groups=mesh['grp'=4,'col'=8] {'col'}, dimensions={1} | all-to-all | bytes 3145728 | tf_op jit(solution)/shard_map/all_to_all | solution.py:51
  487.3 47.8 %all-gather.6.cloned.1.call-done = bf16[24576,128]{1,0:T(8,128)(2,1)} async-done(((bf16[6144,128]{1,0:T(8,128)(2,1)}), bf16[24576,128]{1,0:T(8,128)(2,1)}) %all-gather.6.cloned.1.call-update) | async-done | bytes 6291472 | tf_op jit(solution)/shard_map/all_gather | solution.py:52
  535.1 19.7 %gather_fusion = bf16[384,128,128]{2,1,0:T(8,128)(2,1)} fusion(bf16[4,48,128,128]{3,2,1,0:T(8,128)(2,1)} %bitcast.155, s32[384]{0:T(512)S(1)} %reshape.147), kind=kCustom, calls=%fused_computation | custom fusion | bytes 25168896 | tf_op jit(solution)/shard_map/gather | solution.py:23
  554.8 10.6 broadcast_select_fusion
  565.4 16.5 %copy.32 = bf16[96,128,4,128]{1,0,3,2:T(8,128)(2,1)} copy(bf16[96,128,4,128]{3,1,0,2:T(8,128)(2,1)} %broadcast_select_fusion) | data formatting | bytes 25165824 | tf_op jit(solution)/shard_map/jit(_where)/select_n | solution.py:24
  581.9 9.5 copy.38
  593.4 23.6 %all_to_all.29 = bf16[8,1536,512]{1,0,2:T(8,128)(2,1)} reshape(bf16[96,128,4,128]{1,0,3,2:T(8,128)(2,1)} %copy.32) | data formatting | bytes 25165824 | tf_op jit(solution)/shard_map/all_to_all | solution.py:61
  617.0 12.9 copy.34
  629.9 6.0 all-to-all-start.1
  640.3 377.6 %all-to-all-done.1 = bf16[8,1536,512]{1,2,0:T(8,128)(2,1)} async-done(((bf16[8,1536,512]{1,2,0:T(8,128)(2,1)}), bf16[8,1536,512]{1,2,0:T(8,128)(2,1)}, u32[]{:S(2)}, u32[]{:S(2)}) %all-to-all-start.1) | async-done | bytes 12582944 | tf_op jit(solution)/shard_map/all_to_all | solution.py:61
  1017.9 226.9 %all-gather.8.cloned.1.call-done = bf16[3072,4096]{0,1:T(8,128)(2,1)} async-done(((bf16[3072,512]{0,1:T(8,128)(2,1)}), bf16[3072,4096]{0,1:T(8,128)(2,1)}) %all-gather.8.cloned.1.call-update) | async-done | bytes 25165840 | tf_op jit(solution)/shard_map/all_gather | solution.py:64
  1244.8 48.9 %convolution_subtract_fusion = f32[3072,1536]{1,0:T(8,128)} fusion(f32[3072,1536]{1,0:T(8,128)} %param.6, bf16[3072,4096]{0,1:T(8,128)(2,1)} %all-gather.8.cloned.1.call-done, bf16[1536,4096]{0,1:T(8,128)(2,1)} %bitcast.40), kind=kOutput, calls=%fused_computation.3 | convolution fusion | flops 38659424256 | bytes 75497472 | tf_op jit(solution)/shard_map/dot_general | solution.py:63
  (115 shorter events, 111.6 us)
Async XLA Ops:
  7.2 74.9 %all-gather.4.cloned.1.call-start = ((), (), s32[]{:S(2)}) async-start(), calls=%async_computation.2 | async-start | bytes 4718592 | tf_op jit(solution)/shard_map/all_gather | solution.py:33
  9.3 525.9 %all-gather.6.cloned.1.call-start = ((), (), s32[]{:S(2)}) async-start(), calls=%async_computation.3 | async-start | bytes 7864320 | tf_op jit(solution)/shard_map/all_gather | solution.py:52
  91.8 1.9 copy-start
  297.2 116.2 %copy-start.3 = (f32[768,1024]{1,0:T(8,128)S(1)}, f32[768,1024]{1,0:T(8,128)}, u32[]{:S(2)}) copy-start(f32[768,1024]{1,0:T(8,128)} %param.5) | copy-start | bytes 9437188
  413.4 3.2 copy-start.4
  438.9 46.5 %copy-start.1 = (f32[768,1024]{0,1:T(8,128)}, f32[768,1024]{0,1:T(8,128)S(1)}, u32[]{:S(2)}) copy-start(f32[768,1024]{0,1:T(8,128)S(1)} %get-tuple-element.40) | copy-start | bytes 9437188
  485.4 1.6 copy-start.5
  487.0 757.7 %all-gather.8.cloned.1.call-start = ((), (), s32[]{:S(2)}) async-start(), calls=%async_computation.4 | async-start | bytes 28311552 | tf_op jit(solution)/shard_map/all_gather | solution.py:64
  629.9 6.0 copy-start.2
  629.9 387.9 %all-to-all-start.1 = ((bf16[8,1536,512]{1,2,0:T(8,128)(2,1)}), bf16[8,1536,512]{1,2,0:T(8,128)(2,1)}, u32[]{:S(2)}, u32[]{:S(2)}) async-start(bf16[8,1536,512]{1,2,0:T(8,128)(2,1)} %copy.34), calls=%async_computation.1 | async-start | bytes 25165824 | tf_op jit(solution)/shard_map/all_to_all | solution.py:61
Sparse Core Ops, SparseCore 0:
  10.7 71.3 all-gather.3
  487.1 47.9 all-gather.5
  593.5 651.2 all-gather.7
where the time goes:
time: 1310 us; the launch traced here: 1300 us
  waiting for transfers between devices  725 us (55%)
  other arithmetic  275 us (21%)
  local copies, waits for them, and re-layouts  132 us (10%)
  matrix products  103 us (8%)
  blocking collectives  40 us (3%)
  between operations  19.4 us (1%)
    all_to_all x1, waiting for transfers between devices, on_device(): lax.all_to_all(every_part, 'col', split_axis=0, concat_axis=1, tiled=True)  378 us
    all_gather x1, waiting for transfers between devices, on_device(): lax.all_gather(row_part, 'col', axis=1, tiled=True)  227 us
    another operation x30, other arithmetic, on_device(): factor = jnp.linalg.cholesky(gathered)  173 us
    another operation x3, other arithmetic, on_device(): lax.linalg.triangular_solve(factor, coupling, left_side=False, lower=True...  87.1 us
    all_gather x1, waiting for transfers between devices, on_device(): gathered = lax.all_gather(diag_blocks, 'col', axis=1, tiled=True)  72.7 us
    dot_general x1, matrix products, on_device(): lax.dot_general(lax.all_gather(row_part, 'col', axis=1, tiled=True), col_...  48.9 us
    all_gather x1, waiting for transfers between devices, on_device(): panel_slab = lax.all_gather(panel_tiles, 'grp', axis=0, tiled=True)  47.8 us
    all_to_all x1, blocking collectives, on_device(): lax.all_to_all(panel_half, 'col', split_axis=1, concat_axis=0, tiled=True)  40 us
  transfers between devices with their start and end apart: 4, of which 4 were waited for; matrix products, arithmetic and copies ran while one was open for 1% of the time, Pallas kernels for 0%

commit v1 on v0

--- a/solution.py
+++ b/solution.py
@@ -7,6 +7,29 @@
 BLK = 128
 SBLK = 48
 PBLK = 96
+
+
+def cut_along(shard, dim, count):
+    lengths = shard.shape
+    tiles = shard.reshape(*lengths[:dim], count, lengths[dim] // count, *lengths[dim + 1 :])
+    return jnp.moveaxis(tiles, dim, 0)
+
+
+def in_order(pieces, dim):
+    dims = list(pieces.shape[1:])
+    dims[dim] *= pieces.shape[0]
+    return jnp.moveaxis(pieces, 0, dim).reshape(dims)
+
+
+def exchange_directly(x, axis, split_dim, concat_dim):
+    size, mine = (lax.axis_size(axis), lax.axis_index(axis))
+    parts = cut_along(x, split_dim, size)
+    outs = [parts[mine]]
+    for step in range(1, size):
+        sent = parts[(mine + step) % size]
+        outs.append(lax.ppermute(sent, axis, [(i, (i + step) % size) for i in range(size)]))
+    parts = jnp.stack(outs)[(mine - jnp.arange(size)) % size]
+    return in_order(parts, concat_dim)
 
 
 def swapped(block, axis, stride):
@@ -58,7 +81,7 @@
     row_count = parent_front.shape[0]
     contract = (((1,), (1,)), ((), ()))
     every_part = place_rows(slab_blocks, source_block, present_count, PBLK)
-    col_operand = lax.all_to_all(every_part, "col", split_axis=0, concat_axis=1, tiled=True)
+    col_operand = exchange_directly(every_part, "col", 0, 1)
     row_part = lax.dynamic_slice_in_dim(every_part, grp_index * row_count, row_count, 0)
     update = lax.dot_general(
         lax.all_gather(row_part, "col", axis=1, tiled=True),

time: 1310 us -> 1310 us (level)
  waiting for transfers between devices: 725 us -> 577 us
  local copies, waits for them, and re-layouts: 132 us -> 274 us
    all_to_all x1 -> x0, waiting for transfers between devices: 378 us -> none  [on_device(): lax.all_to_all(every_part, 'col', split_axis=0, concat_axis=1, tiled=True)]
    ppermute x0 -> x7, waiting for transfers between devices: none -> 371 us  [exchange_directly(): lax.ppermute(sent, axis, [(i, (i + step) % size) for i in range(size)])]
    all_gather x1, waiting for transfers between devices: 227 us -> 85.3 us  [on_device(): lax.all_gather(row_part, 'col', axis=1, tiled=True)]
    dynamic_slice x0 -> x8, local copies, waits for them, and re-layouts: none -> 99.2 us  [exchange_directly(): sent = parts[(mine + step) % size]]
    all_to_all x2 -> x0, local copies, waits for them, and re-layouts: 36.5 us -> none  [on_device(): lax.all_to_all(every_part, 'col', split_axis=0, concat_axis=1, tiled=True)]
    unnamed x22 -> x32, local copies, waits for them, and re-layouts: 16.6 us -> 43.4 us
    another operation x24 -> x26, local copies, waits for them, and re-layouts: 29 us -> 53.9 us
    transpose x0 -> x1, local copies, waits for them, and re-layouts: none -> 16.7 us  [in_order(): return jnp.moveaxis(pieces, 0, dim).reshape(dims)]
  transfers between devices with their start and end apart: 4 -> 10, of which waited for: 4 -> 6; matrix products, arithmetic and copies ran while one was open for 1% -> 14% of each run, Pallas kernels for 0% -> 0%
where the time goes in v1:
time: 1310 us; the launch traced here: 1290 us
  waiting for transfers between devices  577 us (44%)
  other arithmetic  275 us (21%)
  local copies, waits for them, and re-layouts  274 us (21%)
  matrix products  103 us (8%)
  blocking collectives  40 us (3%)
  between operations  19.5 us (1%)
    ppermute x7, waiting for transfers between devices, exchange_directly(): lax.ppermute(sent, axis, [(i, (i + step) % size) for i in range(size)])  371 us
    another operation x30, other arithmetic, on_device(): factor = jnp.linalg.cholesky(gathered)  173 us
    dynamic_slice x8, local copies, waits for them, and re-layouts, exchange_directly(): sent = parts[(mine + step) % size]  99.2 us
    another operation x3, other arithmetic, on_device(): lax.linalg.triangular_solve(factor, coupling, left_side=False, lower=True...  87.1 us
    all_gather x1, waiting for transfers between devices, on_device(): lax.all_gather(row_part, 'col', axis=1, tiled=True)  85.3 us
    all_gather x1, waiting for transfers between devices, on_device(): gathered = lax.all_gather(diag_blocks, 'col', axis=1, tiled=True)  72.7 us
    dot_general x1, matrix products, on_device(): lax.dot_general(lax.all_gather(row_part, 'col', axis=1, tiled=True), col_...  48.9 us
    all_gather x1, waiting for transfers between devices, on_device(): panel_slab = lax.all_gather(panel_tiles, 'grp', axis=0, tiled=True)  47.8 us
  transfers between devices with their start and end apart: 10, of which 6 were waited for; matrix products, arithmetic and copies ran while one was open for 14% of the time, Pallas kernels for 0%

profile of v1, /device:TPU:29, one launch (start us, length us, event | category | flops | bytes accessed | tf_op | source)
XLA Modules:
  0.0 1293.7 jit_solution(10451000181351621414)
XLA Ops:
  9.3 72.7 %all-gather.4.cloned.1.call-done = f32[1024,1024]{0,1:T(8,128)} async-done(((f32[1024,128]{0,1:T(8,128)}), f32[1024,1024]{0,1:T(8,128)}) %all-gather.4.cloned.1.call-update) | async-done | bytes 4194320 | tf_op jit(solution)/shard_map/all_gather | solution.py:56
  93.7 11.7 cholesky.223
  105.5 9.8 custom-call.62
  121.7 12.2 cholesky.244
  134.5 9.8 custom-call.63
  147.6 11.7 cholesky.468
  160.7 9.8 custom-call.64
  174.0 11.8 cholesky.487
  187.2 9.8 custom-call.65
  200.4 11.7 cholesky.506
  213.4 10.0 custom-call.66
  226.7 11.7 cholesky.526
  239.7 9.8 custom-call.67
  252.5 12.1 cholesky.546
  265.9 9.8 custom-call.68
  278.5 11.7 cholesky.564
  304.1 29.0 %while.1 = (s32[]{:T(128)}, f32[1024,1024]{1,0:T(8,128)}, s32[8,2]{0,1:T(2,128)S(1)}, f32[8,128,128]{2,1,0:T(8,128)}, s32[]{:T(128)}) while((s32[]{:T(128)}, f32[1024,1024]{1,0:T(8,128)}, s32[8,2]{0,1:T(2,128)S(1)}, f32[8,128,128]{2,1,0:T(8,128)}, s32[]{:T(128)}) %tuple.78), condition=%wide.while_cond, body=%wide.while_body.sunk | while | flops 2 | bytes 132705 | solution.py:70
  333.2 80.2 %custom-call.69 = f32[8,128,128]{1,2,0:T(8,128)} custom-call(f32[8,128,128]{2,1,0:T(8,128)} %get-tuple-element.10), custom_call_target="InvertDiagBlocksLowerTriangular" | custom-call | tf_op jit(solution)/shard_map/triangular_solve | solution.py:70
  445.4 40.0 %all_to_all.16 = bf16[768,8,128]{0,2,1:T(8,128)(2,1)S(1)} all-to-all(bf16[768,8,128]{0,2,1:T(8,128)(2,1)S(1)} %get-tuple-element.108), channel_id=1, replica_groups=mesh['grp'=4,'col'=8] {'col'}, dimensions={1} | all-to-all | bytes 3145728 | tf_op jit(solution)/shard_map/all_to_all | solution.py:74
  487.3 47.8 %all-gather.6.cloned.1.call-done = bf16[24576,128]{1,0:T(8,128)(2,1)} async-done(((bf16[6144,128]{1,0:T(8,128)(2,1)}), bf16[24576,128]{1,0:T(8,128)(2,1)}) %all-gather.6.cloned.1.call-update) | async-done | bytes 6291472 | tf_op jit(solution)/shard_map/all_gather | solution.py:75
  535.1 19.7 %gather_fusion = bf16[384,128,128]{2,1,0:T(8,128)(2,1)} fusion(bf16[4,48,128,128]{3,2,1,0:T(8,128)(2,1)} %bitcast.178, s32[384]{0:T(512)S(1)} %reshape.196), kind=kCustom, calls=%fused_computation | custom fusion | bytes 25168896 | tf_op jit(solution)/shard_map/gather | solution.py:46
  554.8 10.6 broadcast_select_fusion
  565.4 16.5 %copy.33 = bf16[96,128,4,128]{1,0,3,2:T(8,128)(2,1)} copy(bf16[96,128,4,128]{3,1,0,2:T(8,128)(2,1)} %broadcast_select_fusion) | data formatting | bytes 25165824 | tf_op jit(solution)/shard_map/jit(_where)/select_n | solution.py:47
  593.5 23.6 %reshape_reshape.3 = bf16[8,1536,512]{1,0,2:T(8,128)(2,1)} reshape(bf16[96,128,4,128]{1,0,3,2:T(8,128)(2,1)} %copy.33) | data formatting | bytes 25165824 | tf_op jit(solution)/shard_map/reshape;reshape | solution.py:14
  617.1 44.1 %constant_dynamic-slice_fusion.2 = (bf16[1,1536,512]{1,0,2:T(2,128)(2,1)S(1)}, bf16[1,1536,512]{1,0,2:T(2,128)(2,1)}, bf16[1,1536,512]{1,0,2:T(2,128)(2,1)}, bf1...) fusion(bf16[8,1536,512]{1,0,2:T(8,128)(2,1)} %reshape_reshape.3, ...), kind=kLoop, calls=%fused_computation.165 | loop fusion | bytes 25165856 | tf_op jit(solution)/shard_map/dynamic_slice | solution.py:29
  738.6 68.6 %collective-permute-done = bf16[1536,512]{1,0:T(8,128)(2,1)} collective-permute-done((bf16[1536,512]{1,0:T(8,128)(2,1)}, bf16[1536,512]{1,0:T(8,128)(2,1)}, u32[]{:S(2)}, u32[]{:S(2)}) %collective-permute-start) | collective-permute-done | bytes 1572896 | tf_op jit(solution)/shard_map/ppermute | solution.py:30
  815.2 218.1 %collective-permute-done.3 = bf16[1536,512]{1,0:T(8,128)(2,1)} collective-permute-done((bf16[1536,512]{1,0:T(8,128)(2,1)}, bf16[1536,512]{1,0:T(8,128)(2,1)}, u32[]{:S(2)}, u32[]{:S(2)}) %collective-permute-start.3) | collective-permute-done | bytes 1572896 | tf_op jit(solution)/shard_map/ppermute | solution.py:30
  1035.9 84.0 %collective-permute-done.4 = bf16[1536,512]{1,0:T(8,128)(2,1)} collective-permute-done((bf16[1536,512]{1,0:T(8,128)(2,1)}, bf16[1536,512]{1,0:T(8,128)(2,1)}, u32[]{:S(2)}, u32[]{:S(2)}) %collective-permute-start.4) | collective-permute-done | bytes 1572896 | tf_op jit(solution)/shard_map/ppermute | solution.py:30
  1125.1 10.9 gather_fusion.1
  1136.0 16.7 %copy.43 = bf16[1536,8,512]{0,2,1:T(8,128)(2,1)} copy(bf16[1536,8,512]{2,0,1:T(8,128)(2,1)} %bitcast.177) | data formatting | bytes 25165824 | tf_op jit(solution)/shard_map/transpose | solution.py:21
  1152.7 85.3 %all-gather.8.cloned.1.call-done = bf16[3072,4096]{0,1:T(8,128)(2,1)} async-done(((bf16[3072,512]{0,1:T(8,128)(2,1)}), bf16[3072,4096]{0,1:T(8,128)(2,1)}) %all-gather.8.cloned.1.call-update) | async-done | bytes 25165840 | tf_op jit(solution)/shard_map/all_gather | solution.py:87
  1238.1 48.9 %convolution_subtract_fusion = f32[3072,1536]{1,0:T(8,128)} fusion(f32[3072,1536]{1,0:T(8,128)} %param.6, bf16[3072,4096]{0,1:T(8,128)(2,1)} %all-gather.8.cloned.1.call-done, bf16[1536,4096]{0,1:T(8,128)(2,1)} %bitcast.180), kind=kOutput, calls=%fused_computation.4 | convolution fusion | flops 38659424256 | bytes 75497472 | tf_op jit(solution)/shard_map/dot_general | solution.py:86
  (149 shorter events, 222.8 us)
Async XLA Ops:
  7.2 74.9 %all-gather.4.cloned.1.call-start = ((), (), s32[]{:S(2)}) async-start(), calls=%async_computation.1 | async-start | bytes 4718592 | tf_op jit(solution)/shard_map/all_gather | solution.py:56
  9.3 525.9 %all-gather.6.cloned.1.call-start = ((), (), s32[]{:S(2)}) async-start(), calls=%async_computation.2 | async-start | bytes 7864320 | tf_op jit(solution)/shard_map/all_gather | solution.py:75
  91.8 1.9 copy-start
  297.2 116.2 %copy-start.2 = (f32[768,1024]{1,0:T(8,128)S(1)}, f32[768,1024]{1,0:T(8,128)}, u32[]{:S(2)}) copy-start(f32[768,1024]{1,0:T(8,128)} %param.5) | copy-start | bytes 9437188
  413.4 3.2 copy-start.5
  438.9 46.5 %copy-start.1 = (f32[768,1024]{0,1:T(8,128)}, f32[768,1024]{0,1:T(8,128)S(1)}, u32[]{:S(2)}) copy-start(f32[768,1024]{0,1:T(8,128)S(1)} %get-tuple-element.45) | copy-start | bytes 9437188
  485.4 1.6 copy-start.6
  487.0 751.0 %all-gather.8.cloned.1.call-start = ((), (), s32[]{:S(2)}) async-start(), calls=%async_computation.3 | async-start | bytes 28311552 | tf_op jit(solution)/shard_map/all_gather | solution.py:87
  669.4 137.8 %collective-permute-start = (bf16[1536,512]{1,0:T(8,128)(2,1)}, bf16[1536,512]{1,0:T(8,128)(2,1)}, u32[]{:S(2)}, u32[]{:S(2)}) collective-permute-start(bf16[1536,512]{1,0:T(8,128)(2,1)} %bitcast.187), channel_id=1, source_target_pairs={{0,1},{1,2},{2,3},{3,4},{4,5},{5,6},{6,7},{7,0},{8,9},{9,10},{10,1... | collective-permute-start | bytes 4718600 | tf_op jit(solution)/shard_map/ppermute | solution.py:30
  677.7 132.1 %collective-permute-start.1 = (bf16[1536,512]{1,0:T(8,128)(2,1)}, bf16[1536,512]{1,0:T(8,128)(2,1)}, u32[]{:S(2)}, u32[]{:S(2)}) collective-permute-start(bf16[1536,512]{1,0:T(8,128)(2,1)} %bitcast.186), channel_id=1, source_target_pairs={{0,2},{1,3},{2,4},{3,5},{4,6},{5,7},{6,0},{7,1},{8,10},{9,11},{10,... | collective-permute-start | bytes 4718600 | tf_op jit(solution)/shard_map/ppermute | solution.py:30
  687.1 125.4 %collective-permute-start.2 = (bf16[1536,512]{1,0:T(8,128)(2,1)}, bf16[1536,512]{1,0:T(8,128)(2,1)}, u32[]{:S(2)}, u32[]{:S(2)}) collective-permute-start(bf16[1536,512]{1,0:T(8,128)(2,1)} %bitcast.188), channel_id=1, source_target_pairs={{0,3},{1,4},{2,5},{3,6},{4,7},{5,0},{6,1},{7,2},{8,11},{9,12},{10,... | collective-permute-start | bytes 4718600 | tf_op jit(solution)/shard_map/ppermute | solution.py:30
  711.0 322.3 %collective-permute-start.3 = (bf16[1536,512]{1,0:T(8,128)(2,1)}, bf16[1536,512]{1,0:T(8,128)(2,1)}, u32[]{:S(2)}, u32[]{:S(2)}) collective-permute-start(bf16[1536,512]{1,0:T(8,128)(2,1)} %bitcast.192), channel_id=1, source_target_pairs={{0,4},{1,5},{2,6},{3,7},{4,0},{5,1},{6,2},{7,3},{8,12},{9,13},{10,... | collective-permute-start | bytes 4718600 | tf_op jit(solution)/shard_map/ppermute | solution.py:30
  720.3 399.7 %collective-permute-start.4 = (bf16[1536,512]{1,0:T(8,128)(2,1)}, bf16[1536,512]{1,0:T(8,128)(2,1)}, u32[]{:S(2)}, u32[]{:S(2)}) collective-permute-start(bf16[1536,512]{1,0:T(8,128)(2,1)} %bitcast.191), channel_id=1, source_target_pairs={{0,5},{1,6},{2,7},{3,0},{4,1},{5,2},{6,3},{7,4},{8,13},{9,14},{10,... | collective-permute-start | bytes 4718600 | tf_op jit(solution)/shard_map/ppermute | solution.py:30
  735.7 71.4 %copy-start.4 = (bf16[1,1536,512]{2,1,0:T(8,128)(2,1)S(1)}, bf16[1,1536,512]{2,1,0:T(8,128)(2,1)}, u32[]{:S(2)}) copy-start(bf16[1,1536,512]{2,1,0:T(8,128)(2,1)} %copy.41) | copy-start | bytes 4718596
  735.7 74.1 %copy-start.3 = (bf16[1,1536,512]{2,1,0:T(8,128)(2,1)S(1)}, bf16[1,1536,512]{2,1,0:T(8,128)(2,1)}, u32[]{:S(2)}) copy-start(bf16[1,1536,512]{2,1,0:T(8,128)(2,1)} %copy.42) | copy-start | bytes 4718596
  807.2 315.4 %collective-permute-start.5 = (bf16[1536,512]{1,0:T(8,128)(2,1)S(1)}, bf16[1536,512]{1,0:T(8,128)(2,1)S(1)}, u32[]{:S(2)}, u32[]{:S(2)}) collective-permute-start(bf16[1536,512]{1,0:T(8,128)(2,1)S(1)} %bitcast.190), channel_id=1, source_target_pairs={{0,6},{1,7},{2,0},{3,1},{4,2},{5,3},{6,4},{7,5},{8,14},{9,15},{10,... | collective-permute-start | bytes 4718600 | tf_op jit(solution)/shard_map/ppermute | solution.py:30
  809.8 314.0 %collective-permute-start.6 = (bf16[1536,512]{1,0:T(8,128)(2,1)S(1)}, bf16[1536,512]{1,0:T(8,128)(2,1)S(1)}, u32[]{:S(2)}, u32[]{:S(2)}) collective-permute-start(bf16[1536,512]{1,0:T(8,128)(2,1)S(1)} %bitcast.189), channel_id=1, source_target_pairs={{0,7},{1,0},{2,1},{3,2},{4,3},{5,4},{6,5},{7,6},{8,15},{9,8},{10,9... | collective-permute-start | bytes 4718600 | tf_op jit(solution)/shard_map/ppermute | solution.py:30
Sparse Core Ops, SparseCore 0:
  10.7 71.3 all-gather.3
  487.1 47.9 all-gather.5
  593.5 644.5 all-gather.7
